TPU v7x, 512 devices: a whole 4x8x8 slice. The times are simulated.
512 devices in a mesh: inp: 128 (over y, z, core), vis: 4 (over x).
Axes of the slice: x: 4, y: 8, z: 8, core: 2. Of those that a mesh axis runs over, the one named last changes fastest.
Arguments:
- samples: bfloat16 [128, 2048, 2048], P('vis', 'inp'), may hold values from -6 to 6
- history: bfloat16 [3, 2048, 2048], P(None, 'inp'), may hold values from -6 to 6
- fir_taps: float32 [4, 2048], replicated, may hold values from -3 to 3
- kept_channels: int32 [128], replicated, may hold values from 0 to 1023, as said below
Outputs:
- visibility: bfloat16 [128, 2048, 2048], P('inp', 'vis')
Inputs may be any that keep to these rules, and one draw needn't show every extreme that they name: `kept_channels`: 128 distinct channel numbers in no particular order; channels 0 and 1023 are always among them.
All inputs are finite; a program needn't handle non-finite values.
Results may differ from a plain program's by a relative error of at most 0.0078.
Values may be sent and summed in bfloat16 or wider, within the bound.
A program may use at most 64 MiB of HBM per device.

v0:
```python
from functools import partial
import math
import jax
import jax.numpy as jnp
from jax import lax
from jax.sharding import PartitionSpec as P

TAPS = 4
CH_DEV = 1


def shifted(value, axis, steps):
    count = lax.axis_size(axis)
    initial, last = (max(0, -steps), min(count, count - steps))
    return lax.ppermute(value, axis, [(source, source + steps) for source in range(initial, last)])


def make_table(kept_channels, sample_count):
    positions = jnp.arange(sample_count, dtype=jnp.int32)
    products = kept_channels[:, None] * positions[None, :] % sample_count
    angles = products.astype(jnp.float32) * (2.0 * math.pi / sample_count)
    norm_scale = 1.0 / math.sqrt(sample_count)
    table = jnp.concatenate([jnp.cos(angles) * norm_scale, -jnp.sin(angles) * norm_scale], axis=0)
    return table.astype(jnp.bfloat16)


def add_frames(running, shard_piece, offset, vis_index, row_count):
    real_part = shard_piece[0]
    imag_part = shard_piece[1]
    stacked = jnp.concatenate([real_part, imag_part], axis=1)
    rotated = jnp.concatenate([-imag_part, real_part], axis=1)
    row_block = lax.dynamic_slice_in_dim(stacked, vis_index * row_count, row_count, 2)
    input_total = stacked.shape[2]
    re_block = jnp.einsum("cfa,cfb->cab", row_block, stacked, preferred_element_type=jnp.float32)
    im_block = jnp.einsum("cfa,cfb->cab", row_block, rotated, preferred_element_type=jnp.float32)
    row_ids = vis_index * row_count + jnp.arange(row_count, dtype=jnp.int32)
    col_ids = jnp.arange(input_total, dtype=jnp.int32)
    contribution = jnp.where(col_ids[None, None, :] >= row_ids[None, :, None], re_block, im_block)
    return contribution


def per_device(samples, history, fir_taps, kept_channels):
    vis_count = lax.axis_size("vis")
    vis_index = lax.axis_index("vis")
    inp_count = lax.axis_size("inp")
    frame_count, input_count, sample_count = samples.shape
    history_len = TAPS - 1
    previous = shifted(samples[frame_count - history_len :], "vis", 1)
    previous = jnp.where(vis_index == 0, history, previous)
    extended = jnp.concatenate([previous, samples], axis=0)
    weighted = fir_taps[0][None, None, :] * extended[0:frame_count].astype(jnp.float32)
    for tap_index in range(1, TAPS):
        weighted = weighted + fir_taps[tap_index][None, None, :] * extended[
            tap_index : tap_index + frame_count
        ].astype(jnp.float32)
    weighted = weighted.astype(jnp.bfloat16)
    dft_table = make_table(kept_channels, sample_count)
    kept_total = kept_channels.shape[0]
    spectra = jnp.einsum(
        "kn,fin->kfi", dft_table, weighted, preferred_element_type=jnp.float32
    ).astype(jnp.bfloat16)
    spectra = spectra.reshape(2, kept_total, frame_count, input_count)
    input_total = input_count * inp_count
    row_count = input_total // vis_count
    frame_total = frame_count * vis_count
    initial = jnp.zeros((CH_DEV, row_count, input_total), jnp.float32)
    correlate = partial(add_frames, vis_index=vis_index, row_count=row_count)
    all_frames = lax.all_gather(spectra, "vis", axis=2, tiled=True)
    channel_data = lax.all_to_all(all_frames, "inp", split_axis=1, concat_axis=3, tiled=True)
    summed = correlate(initial, channel_data, 0)
    return (summed / float(frame_total)).astype(jnp.bfloat16)


def solution(mesh):
    return jax.shard_map(
        per_device,
        mesh=mesh,
        in_specs=(P("vis", "inp", None), P(None, "inp", None), P(), P()),
        out_specs=P("inp", "vis", None),
        check_vma=False,
    )
```

profile of v0, /device:TPU:1, one launch (start us, length us, event | category | flops | bytes accessed | tf_op | source)
XLA Modules:
  0.0 116.5 jit_solution(1827298505399509753)
XLA Ops:
  6.5 0.0 copy-start
  6.5 0.0 all-gather.2.cloned.1.call-start
  6.5 1.1 slice.33
  7.6 4.0 %collective-permute-start = (bf16[3,16,2048]{2,1,0:T(8,128)(2,1)S(1)}, bf16[3,16,2048]{2,1,0:T(8,128)(2,1)S(1)}, u32[]{:S(2)}, u32[]{:S(2)}) collective-permute-start(bf16[3,16,2048]{2,1,0:T(8,128)(2,1)S(1)} %slice.33), channel_id=1, source_target_pairs={{0,1},{1,2},{2,3},{4,5},{5,6},{6,7},{8,9},{9,10},{10,11},{12,13},{... | collective-permute-start | bytes 589832 | tf_op jit(solution)/shard_map/ppermute | solution.py:15
  11.6 5.6 %multiply_convert_fusion.2 = (bf16[128,2048]{1,0:T(8,128)(2,1)S(1)}, bf16[128,2048]{1,0:T(8,128)(2,1)S(1)}) fusion(s32[128]{0:T(128)} %param.7), kind=kLoop, calls=%fused_computation.33 | loop fusion | flops 4980736 | bytes 1049088 | tf_op jit(solution)/shard_map/convert
  17.2 1.5 %fusion.29 = (f32[1,2048]{1,0:T(1,128)S(1)}, f32[1,2048]{1,0:T(1,128)S(1)}, f32[1,2048]{1,0:T(1,128)}, f32[1,2048]{1,0:T(1,128)}) fusion(f32[4,2048]{1,0:T(4,128)} %param.6), kind=kLoop, calls=%fused_computation.46 | loop fusion | bytes 65536 | tf_op jit(solution)/shard_map/slice | solution.py:51
  18.8 0.0 collective-permute-done
  18.8 1.0 broadcast_select_fusion
  19.7 0.0 copy-done
  19.7 2.7 %add_convert_fusion = bf16[32,16,2048]{2,1,0:T(8,128)(2,1)S(1)} fusion(bf16[32,16,2048]{2,1,0:T(8,128)(2,1)S(1)} %copy-done, bf16[3,16,2048]{2,1,0:T(8,128)(2,1)S(1)} %broadcast_select_fusion, f32[2048]{0:T(1024)} %bitcast.36, f32[2048]{0:T(1024)} %bitcast.37, f32[2048]{0:T(1024)S(1)} %bitcast.35, f32[2048]{0:T(1024)S(1)} %bitcast.34), kind=kLoop, calls=%fused_computation.1 | loop fusion | flops 15728640 | bytes 4423680 | tf_op jit(solution)/shard_map/convert_element_type | solution.py:56
  22.5 1.6 %fusion.5 = bf16[256,32,16]{0,1,2:T(8,128)(2,1)S(1)} fusion(bf16[32,16,2048]{2,1,0:T(8,128)(2,1)S(1)} %add_convert_fusion, bf16[128,2048]{1,0:T(8,128)(2,1)S(1)} %get-tuple-element.12, bf16[128,2048]{1,0:T(8,128)(2,1)S(1)} %get-tuple-element.11), kind=kOutput, calls=%fused_computation.16 | convolution fusion | flops 539099136 | bytes 3407872 | tf_op jit(solution)/shard_map/kn,fin->kfi/dot_general | solution.py:59
  24.1 0.1 reshape.47
  24.2 1.0 copy.9
  25.2 0.0 all-gather.2.cloned.1.call-update
  25.2 32.2 %all-gather.2.cloned.1.call-done = bf16[2,128,128,16]{1,3,0,2:T(8,128)(2,1)} async-done(((bf16[2,128,32,16]{1,3,0,2:T(8,128)(2,1)}), bf16[2,128,128,16]{1,3,0,2:T(8,128)(2,1)}) %all-gather.2.cloned.1.call-update) | async-done | bytes 1048592 | tf_op jit(solution)/shard_map/all_gather | solution.py:68
  57.5 3.2 %copy.10 = bf16[2,128,128,16]{2,3,0,1:T(8,128)(2,1)} copy(bf16[2,128,128,16]{1,3,0,2:T(8,128)(2,1)} %all-gather.2.cloned.1.call-done) | data formatting | bytes 2097152 | tf_op jit(solution)/shard_map/all_gather | solution.py:68
  60.7 15.2 %all-to-all-start = ((bf16[2,128,128,16]{2,3,0,1:T(8,128)(2,1)}), bf16[2,128,128,16]{2,3,0,1:T(8,128)(2,1)S(1)}, u32[]{:S(2)}, u32[]{:S(2)}) async-start(bf16[2,128,128,16]{2,3,0,1:T(8,128)(2,1)} %copy.10), calls=%async_computation | async-start | bytes 2097152 | tf_op jit(solution)/shard_map/all_to_all | solution.py:69
  75.9 30.4 %all-to-all-done = bf16[2,128,128,16]{2,3,0,1:T(8,128)(2,1)S(1)} async-done(((bf16[2,128,128,16]{2,3,0,1:T(8,128)(2,1)}), bf16[2,128,128,16]{2,3,0,1:T(8,128)(2,1)S(1)}, u32[]{:S(2)}, u32[]{:S(2)}) %all-to-all-start) | async-done | bytes 1048608 | tf_op jit(solution)/shard_map/all_to_all | solution.py:69
  106.3 0.2 copy.17
  106.5 0.2 fusion.28
  106.7 0.1 bitcast_negate_fusion
  106.8 0.7 fusion.9
  107.5 2.1 %fusion = bf16[1,512,2048]{2,1,0:T(8,128)(2,1)} fusion(f32[512,2048]{1,0:T(8,128)S(1)} %fusion.9, s32[512]{0:T(512)S(1)} %iota_add_fusion, bf16[1,128,2048]{1,2,0:T(8,128)(2,1)S(1)} %bitcast.30, bf16[1,128,2048]{1,2,0:T(8,128)(2,1)S(1)} %bitcast_negate_fusion, s32[]{:T(128)S(6)} %select_n.26, bf16[1,128,2048]{1,2,0:T(8,128)(2,1)S(1)} %bitcast.32), kind=kOutput, calls=%fused_computation.5 | convolution fusion | flops 543686656 | bytes 8390660 | tf_op jit(solution)/shard_map/cfa,cfb->cab/dot_general | solution.py:35
  (1 shorter events, 0.0 us)
Async XLA Ops:
  6.5 13.2 %copy-start = (bf16[32,16,2048]{2,1,0:T(8,128)(2,1)S(1)}, bf16[32,16,2048]{2,1,0:T(8,128)(2,1)}, u32[]{:S(2)}) copy-start(bf16[32,16,2048]{2,1,0:T(8,128)(2,1)} %param.4) | copy-start | bytes 6291460
  6.5 50.9 %all-gather.2.cloned.1.call-start = ((), (), s32[]{:S(2)}) async-start(), calls=%async_computation.1 | async-start | bytes 1310720 | tf_op jit(solution)/shard_map/all_gather | solution.py:68
  7.6 11.1 %collective-permute-start = (bf16[3,16,2048]{2,1,0:T(8,128)(2,1)S(1)}, bf16[3,16,2048]{2,1,0:T(8,128)(2,1)S(1)}, u32[]{:S(2)}, u32[]{:S(2)}) collective-permute-start(bf16[3,16,2048]{2,1,0:T(8,128)(2,1)S(1)} %slice.33), channel_id=1, source_target_pairs={{0,1},{1,2},{2,3},{4,5},{5,6},{6,7},{8,9},{9,10},{10,11},{12,13},{... | collective-permute-start | bytes 589832 | tf_op jit(solution)/shard_map/ppermute | solution.py:15
  60.7 45.6 %all-to-all-start = ((bf16[2,128,128,16]{2,3,0,1:T(8,128)(2,1)}), bf16[2,128,128,16]{2,3,0,1:T(8,128)(2,1)S(1)}, u32[]{:S(2)}, u32[]{:S(2)}) async-start(bf16[2,128,128,16]{2,3,0,1:T(8,128)(2,1)} %copy.10), calls=%async_computation | async-start | bytes 2097152 | tf_op jit(solution)/shard_map/all_to_all | solution.py:69
Sparse Core Ops, SparseCore 0:
  25.4 32.0 all-gather.1
where the time goes:
time: 117 us
  waiting for transfers between devices  62.7 us (54%)
  starting transfers between devices  19.2 us (16%)
  between operations  13.5 us (12%)
  other arithmetic  9.41 us (8%)
  local copies, waits for them, and re-layouts  7.24 us (6%)
  matrix products  4.52 us (4%)
    all_gather x1, waiting for transfers between devices, per_device(): all_frames = lax.all_gather(spectra, 'vis', axis=2, tiled=True)  32.2 us
    all_to_all x1, waiting for transfers between devices, per_device(): lax.all_to_all(all_frames, 'inp', split_axis=1, concat_axis=3, tiled=True)  30.4 us
    all_to_all x1, starting transfers between devices, per_device(): lax.all_to_all(all_frames, 'inp', split_axis=1, concat_axis=3, tiled=True)  15.2 us
    another operation x1, other arithmetic  5.62 us
    ppermute x1, starting transfers between devices, shifted(): lax.ppermute(value, axis, [(source, source + steps) for source in range(i...  3.96 us
    all_gather x1, local copies, waits for them, and re-layouts, per_device(): all_frames = lax.all_gather(spectra, 'vis', axis=2, tiled=True)  3.17 us
    convert_element_type x1, other arithmetic, per_device(): weighted = weighted.astype(jnp.bfloat16)  2.74 us
  transfers between devices with their start and end apart: 3, of which 2 were waited for; matrix products, arithmetic and copies ran while one was open for 6% of the time, Pallas kernels for 0%

commit v1 on v0

--- a/solution.py
+++ b/solution.py
@@ -7,6 +7,19 @@
 
 TAPS = 4
 CH_DEV = 1
+
+
+def ring_gather(x, axis, dim):
+    ways = lax.axis_size(axis)
+    up = [(d, (d + 1) % ways) for d in range(ways)]
+    down = [(d, (d - 1) % ways) for d in range(ways)]
+    earlier, later = ([x], [x])
+    for _ in range(ways // 2):
+        earlier.append(lax.ppermute(earlier[-1], axis, up))
+    for _ in range((ways - 1) // 2):
+        later.append(lax.ppermute(later[-1], axis, down))
+    line = jnp.concatenate([*earlier[::-1], *later[1:]], axis=dim)
+    return jnp.roll(line, (lax.axis_index(axis) - ways // 2) * x.shape[dim], axis=dim)
 
 
 def shifted(value, axis, steps):
@@ -65,7 +78,7 @@
     frame_total = frame_count * vis_count
     initial = jnp.zeros((CH_DEV, row_count, input_total), jnp.float32)
     correlate = partial(add_frames, vis_index=vis_index, row_count=row_count)
-    all_frames = lax.all_gather(spectra, "vis", axis=2, tiled=True)
+    all_frames = ring_gather(spectra, "vis", 2)
     channel_data = lax.all_to_all(all_frames, "inp", split_axis=1, concat_axis=3, tiled=True)
     summed = correlate(initial, channel_data, 0)
     return (summed / float(frame_total)).astype(jnp.bfloat16)

time: 117 us -> 95.6 us (0.82)
  waiting for transfers between devices: 62.7 us -> 39.6 us
  starting transfers between devices: 19.2 us -> 34.4 us
  between operations: 13.5 us -> 0.21 us
    all_gather x1 -> x0, waiting for transfers between devices: 32.2 us -> none  [per_device(): all_frames = lax.all_gather(spectra, 'vis', axis=2, tiled=True)]
    ppermute x0 -> x3, waiting for transfers between devices: none -> 9.16 us  [the longest x2 7.92 us: ring_gather(): earlier.append(lax.ppermute(earlier[-1], axis, up))]
    ppermute x0 -> x3, starting transfers between devices: none -> 8.67 us  [the longest x1 4.57 us: ring_gather(): later.append(lax.ppermute(later[-1], axis, down))]
    all_to_all x1, starting transfers between devices: 15.2 us -> 21.8 us  [per_device(): lax.all_to_all(all_frames, 'inp', split_axis=1, concat_axis=3, tiled=True)]
    all_gather x1 -> x0, local copies, waits for them, and re-layouts: 3.17 us -> none  [per_device(): all_frames = lax.all_gather(spectra, 'vis', axis=2, tiled=True)]
    dynamic_slice x0 -> x2, local copies, waits for them, and re-layouts: none -> 2.45 us  [ring_gather(): jnp.roll(line, (lax.axis_index(axis) - ways // 2) * x.shape[dim], axis=dim)]
  transfers between devices with their start and end apart: 3 -> 5, of which waited for: 2 -> 4; matrix products, arithmetic and copies ran while one was open for 6% -> 8% of each run, Pallas kernels for 0% -> 0%
where the time goes in v1:
time: 95.6 us; the launch traced here: 94.4 us
  waiting for transfers between devices  39.6 us (41%)
  starting transfers between devices  34.4 us (36%)
  other arithmetic  9.41 us (10%)
  local copies, waits for them, and re-layouts  6.28 us (7%)
  matrix products  4.52 us (5%)
    all_to_all x1, waiting for transfers between devices, per_device(): lax.all_to_all(all_frames, 'inp', split_axis=1, concat_axis=3, tiled=True)  30.4 us
    all_to_all x1, starting transfers between devices, per_device(): lax.all_to_all(all_frames, 'inp', split_axis=1, concat_axis=3, tiled=True)  21.8 us
    ppermute x2, waiting for transfers between devices, ring_gather(): earlier.append(lax.ppermute(earlier[-1], axis, up))  7.92 us
    another operation x1, other arithmetic  5.62 us
    ppermute x1, starting transfers between devices, ring_gather(): later.append(lax.ppermute(later[-1], axis, down))  4.57 us
    ppermute x2, starting transfers between devices, ring_gather(): earlier.append(lax.ppermute(earlier[-1], axis, up))  4.1 us
    ppermute x1, starting transfers between devices, shifted(): lax.ppermute(value, axis, [(source, source + steps) for source in range(i...  3.96 us
    convert_element_type x1, other arithmetic, per_device(): weighted = weighted.astype(jnp.bfloat16)  2.74 us
  transfers between devices with their start and end apart: 5, of which 4 were waited for; matrix products, arithmetic and copies ran while one was open for 8% of the time, Pallas kernels for 0%

profile of v1, /device:TPU:1, one launch (start us, length us, event | category | flops | bytes accessed | tf_op | source)
XLA Modules:
  0.0 94.4 jit_solution(12487439155053262871)
XLA Ops:
  0.0 0.0 copy-start
  0.0 1.1 %slice.33 = bf16[3,16,2048]{2,1,0:T(8,128)(2,1)S(1)} slice(bf16[32,16,2048]{2,1,0:T(8,128)(2,1)} %param.4), slice={[29:32], [0:16], [0:2048]} | slice | bytes 393216 | tf_op jit(solution)/shard_map/slice | solution.py:61
  1.1 4.0 %collective-permute-start = (bf16[3,16,2048]{2,1,0:T(8,128)(2,1)S(1)}, bf16[3,16,2048]{2,1,0:T(8,128)(2,1)S(1)}, u32[]{:S(2)}, u32[]{:S(2)}) collective-permute-start(bf16[3,16,2048]{2,1,0:T(8,128)(2,1)S(1)} %slice.33), channel_id=1, source_target_pairs={{0,1},{1,2},{2,3},{4,5},{5,6},{6,7},{8,9},{9,10},{10,11},{12,13},{... | collective-permute-start | bytes 589832 | tf_op jit(solution)/shard_map/ppermute | solution.py:28
  5.1 5.6 %multiply_convert_fusion.2 = (bf16[128,2048]{1,0:T(8,128)(2,1)S(1)}, bf16[128,2048]{1,0:T(8,128)(2,1)S(1)}) fusion(s32[128]{0:T(128)} %param.7), kind=kLoop, calls=%fused_computation.33 | loop fusion | flops 4980736 | bytes 1049088 | tf_op jit(solution)/shard_map/convert
  10.7 1.6 %fusion.29 = (f32[1,2048]{1,0:T(1,128)S(1)}, f32[1,2048]{1,0:T(1,128)S(1)}, f32[1,2048]{1,0:T(1,128)}, f32[1,2048]{1,0:T(1,128)}) fusion(f32[4,2048]{1,0:T(4,128)} %param.6), kind=kLoop, calls=%fused_computation.55 | loop fusion | bytes 65536 | tf_op jit(solution)/shard_map/slice | solution.py:64
  12.2 0.0 collective-permute-done
  12.3 1.0 %broadcast_select_fusion = bf16[3,16,2048]{2,1,0:T(8,128)(2,1)S(1)} fusion(bf16[3,16,2048]{2,1,0:T(8,128)(2,1)} %param.5, bf16[3,16,2048]{2,1,0:T(8,128)(2,1)S(1)} %collective-permute-done, pred[]{:T(512)S(6)} %eq.8), kind=kLoop, calls=%fused_computation.39 | loop fusion | flops 98304 | bytes 589825 | tf_op jit(solution)/shard_map/jit(_where)/select_n | solution.py:62
  13.2 0.0 copy-done
  13.2 2.7 %add_convert_fusion = bf16[32,16,2048]{2,1,0:T(8,128)(2,1)S(1)} fusion(bf16[32,16,2048]{2,1,0:T(8,128)(2,1)S(1)} %copy-done, bf16[3,16,2048]{2,1,0:T(8,128)(2,1)S(1)} %broadcast_select_fusion, f32[2048]{0:T(1024)} %bitcast.36, f32[2048]{0:T(1024)} %bitcast.37, f32[2048]{0:T(1024)S(1)} %bitcast.35, f32[2048]{0:T(1024)S(1)} %bitcast.34), kind=kLoop, calls=%fused_computation.1 | loop fusion | flops 15728640 | bytes 4423680 | tf_op jit(solution)/shard_map/convert_element_type | solution.py:69
  16.0 1.6 %fusion.5 = bf16[256,32,16]{0,1,2:T(8,128)(2,1)S(1)} fusion(bf16[32,16,2048]{2,1,0:T(8,128)(2,1)S(1)} %add_convert_fusion, bf16[128,2048]{1,0:T(8,128)(2,1)S(1)} %get-tuple-element.12, bf16[128,2048]{1,0:T(8,128)(2,1)S(1)} %get-tuple-element.11), kind=kOutput, calls=%fused_computation.16 | convolution fusion | flops 539099136 | bytes 3407872 | tf_op jit(solution)/shard_map/kn,fin->kfi/dot_general | solution.py:72
  17.6 0.1 reshape.47
  17.7 0.2 copy.12
  17.9 2.2 %collective-permute-start.1 = (bf16[2,128,32,16]{1,3,2,0:T(8,128)(2,1)S(1)}, bf16[2,128,32,16]{1,3,2,0:T(8,128)(2,1)S(1)}, u32[]{:S(2)}, u32[]{:S(2)}) collective-permute-start(bf16[2,128,32,16]{1,3,2,0:T(8,128)(2,1)S(1)} %copy.12), channel_id=1, source_target_pairs={{0,1},{1,2},{2,3},{3,0},{4,5},{5,6},{6,7},{7,4},{8,9},{9,10},{10,1... | collective-permute-start | bytes 786440 | tf_op jit(solution)/shard_map/ppermute | solution.py:18
  20.1 6.1 %collective-permute-done.1 = bf16[2,128,32,16]{1,3,2,0:T(8,128)(2,1)S(1)} collective-permute-done((bf16[2,128,32,16]{1,3,2,0:T(8,128)(2,1)S(1)}, bf16[2,128,32,16]{1,3,2,0:T(8,128)(2,1)S(1)}, u32[]{:S(2)}, u32[]{:S(2)}) %collective-permute-start.1) | collective-permute-done | bytes 262176 | tf_op jit(solution)/shard_map/ppermute | solution.py:18
  26.2 1.9 %collective-permute-start.2 = (bf16[2,128,32,16]{1,3,2,0:T(8,128)(2,1)S(1)}, bf16[2,128,32,16]{1,3,2,0:T(8,128)(2,1)S(1)}, u32[]{:S(2)}, u32[]{:S(2)}) collective-permute-start(bf16[2,128,32,16]{1,3,2,0:T(8,128)(2,1)S(1)} %collective-permute-done.1), channel_id=1, source_target_pairs={{0,1},{1,2},{2,3},{3,0},{4,5},{5,6},{6,7},{7,4},{8,9},{9,10},{10,1... | collective-permute-start | bytes 786440 | tf_op jit(solution)/shard_map/ppermute | solution.py:18
  28.1 4.6 %collective-permute-start.3 = (bf16[2,128,32,16]{1,3,2,0:T(8,128)(2,1)S(1)}, bf16[2,128,32,16]{1,3,2,0:T(8,128)(2,1)S(1)}, u32[]{:S(2)}, u32[]{:S(2)}) collective-permute-start(bf16[2,128,32,16]{1,3,2,0:T(8,128)(2,1)S(1)} %copy.12), channel_id=1, source_target_pairs={{0,3},{1,0},{2,1},{3,2},{4,7},{5,4},{6,5},{7,6},{8,11},{9,8},{10,9... | collective-permute-start | bytes 786440 | tf_op jit(solution)/shard_map/ppermute | solution.py:20
  32.7 1.8 %collective-permute-done.2 = bf16[2,128,32,16]{1,3,2,0:T(8,128)(2,1)S(1)} collective-permute-done((bf16[2,128,32,16]{1,3,2,0:T(8,128)(2,1)S(1)}, bf16[2,128,32,16]{1,3,2,0:T(8,128)(2,1)S(1)}, u32[]{:S(2)}, u32[]{:S(2)}) %collective-permute-start.2) | collective-permute-done | bytes 262176 | tf_op jit(solution)/shard_map/ppermute | solution.py:18
  34.6 0.2 constant_dynamic-update-slice_fusion.5
  34.8 1.2 %collective-permute-done.3 = bf16[2,128,32,16]{1,3,2,0:T(8,128)(2,1)S(1)} collective-permute-done((bf16[2,128,32,16]{1,3,2,0:T(8,128)(2,1)S(1)}, bf16[2,128,32,16]{1,3,2,0:T(8,128)(2,1)S(1)}, u32[]{:S(2)}, u32[]{:S(2)}) %collective-permute-start.3) | collective-permute-done | bytes 262176 | tf_op jit(solution)/shard_map/ppermute | solution.py:20
  36.1 0.2 constant_dynamic-update-slice_fusion.1
  36.4 0.2 constant_dynamic-slice_fusion
  36.6 2.3 %copy.16 = bf16[2,128,128,16]{2,3,0,1:T(8,128)(2,1)} copy(bf16[2,128,128,16]{1,3,2,0:T(8,128)(2,1)S(1)} %constant_dynamic-slice_fusion) | data formatting | bytes 2097152 | tf_op jit(solution)/shard_map/jit(_roll_dynamic)/dynamic_slice | solution.py:22
  38.8 21.8 %all-to-all-start = ((bf16[2,128,128,16]{2,3,0,1:T(8,128)(2,1)}), bf16[2,128,128,16]{2,3,0,1:T(8,128)(2,1)S(1)}, u32[]{:S(2)}, u32[]{:S(2)}) async-start(bf16[2,128,128,16]{2,3,0,1:T(8,128)(2,1)} %copy.16), calls=%async_computation | async-start | bytes 2097152 | tf_op jit(solution)/shard_map/all_to_all | solution.py:82
  60.6 30.4 %all-to-all-done = bf16[2,128,128,16]{2,3,0,1:T(8,128)(2,1)S(1)} async-done(((bf16[2,128,128,16]{2,3,0,1:T(8,128)(2,1)}), bf16[2,128,128,16]{2,3,0,1:T(8,128)(2,1)S(1)}, u32[]{:S(2)}, u32[]{:S(2)}) %all-to-all-start) | async-done | bytes 1048608 | tf_op jit(solution)/shard_map/all_to_all | solution.py:82
  91.0 0.2 copy.25
  91.2 0.2 fusion.28
  91.4 0.1 bitcast_negate_fusion
  91.5 0.7 fusion.9
  92.3 2.1 %fusion = bf16[1,512,2048]{2,1,0:T(8,128)(2,1)} fusion(f32[512,2048]{1,0:T(8,128)S(1)} %fusion.9, s32[512]{0:T(512)S(1)} %iota_add_fusion, bf16[1,128,2048]{1,2,0:T(8,128)(2,1)S(1)} %bitcast.30, bf16[1,128,2048]{1,2,0:T(8,128)(2,1)S(1)} %bitcast_negate_fusion, s32[]{:T(128)S(6)} %select_n.40, bf16[1,128,2048]{1,2,0:T(8,128)(2,1)S(1)} %bitcast.32), kind=kOutput, calls=%fused_computation.5 | convolution fusion | flops 543686656 | bytes 8390660 | tf_op jit(solution)/shard_map/cfa,cfb->cab/dot_general | solution.py:48
  (7 shorter events, 0.2 us)
Async XLA Ops:
  0.0 13.2 %copy-start = (bf16[32,16,2048]{2,1,0:T(8,128)(2,1)S(1)}, bf16[32,16,2048]{2,1,0:T(8,128)(2,1)}, u32[]{:S(2)}) copy-start(bf16[32,16,2048]{2,1,0:T(8,128)(2,1)} %param.4) | copy-start | bytes 6291460
  1.1 11.2 %collective-permute-start = (bf16[3,16,2048]{2,1,0:T(8,128)(2,1)S(1)}, bf16[3,16,2048]{2,1,0:T(8,128)(2,1)S(1)}, u32[]{:S(2)}, u32[]{:S(2)}) collective-permute-start(bf16[3,16,2048]{2,1,0:T(8,128)(2,1)S(1)} %slice.33), channel_id=1, source_target_pairs={{0,1},{1,2},{2,3},{4,5},{5,6},{6,7},{8,9},{9,10},{10,11},{12,13},{... | collective-permute-start | bytes 589832 | tf_op jit(solution)/shard_map/ppermute | solution.py:28
  17.9 8.3 %collective-permute-start.1 = (bf16[2,128,32,16]{1,3,2,0:T(8,128)(2,1)S(1)}, bf16[2,128,32,16]{1,3,2,0:T(8,128)(2,1)S(1)}, u32[]{:S(2)}, u32[]{:S(2)}) collective-permute-start(bf16[2,128,32,16]{1,3,2,0:T(8,128)(2,1)S(1)} %copy.12), channel_id=1, source_target_pairs={{0,1},{1,2},{2,3},{3,0},{4,5},{5,6},{6,7},{7,4},{8,9},{9,10},{10,1... | collective-permute-start | bytes 786440 | tf_op jit(solution)/shard_map/ppermute | solution.py:18
  26.2 8.3 %collective-permute-start.2 = (bf16[2,128,32,16]{1,3,2,0:T(8,128)(2,1)S(1)}, bf16[2,128,32,16]{1,3,2,0:T(8,128)(2,1)S(1)}, u32[]{:S(2)}, u32[]{:S(2)}) collective-permute-start(bf16[2,128,32,16]{1,3,2,0:T(8,128)(2,1)S(1)} %collective-permute-done.1), channel_id=1, source_target_pairs={{0,1},{1,2},{2,3},{3,0},{4,5},{5,6},{6,7},{7,4},{8,9},{9,10},{10,1... | collective-permute-start | bytes 786440 | tf_op jit(solution)/shard_map/ppermute | solution.py:18
  28.1 7.9 %collective-permute-start.3 = (bf16[2,128,32,16]{1,3,2,0:T(8,128)(2,1)S(1)}, bf16[2,128,32,16]{1,3,2,0:T(8,128)(2,1)S(1)}, u32[]{:S(2)}, u32[]{:S(2)}) collective-permute-start(bf16[2,128,32,16]{1,3,2,0:T(8,128)(2,1)S(1)} %copy.12), channel_id=1, source_target_pairs={{0,3},{1,0},{2,1},{3,2},{4,7},{5,4},{6,5},{7,6},{8,11},{9,8},{10,9... | collective-permute-start | bytes 786440 | tf_op jit(solution)/shard_map/ppermute | solution.py:20
  38.8 52.2 %all-to-all-start = ((bf16[2,128,128,16]{2,3,0,1:T(8,128)(2,1)}), bf16[2,128,128,16]{2,3,0,1:T(8,128)(2,1)S(1)}, u32[]{:S(2)}, u32[]{:S(2)}) async-start(bf16[2,128,128,16]{2,3,0,1:T(8,128)(2,1)} %copy.16), calls=%async_computation | async-start | bytes 2097152 | tf_op jit(solution)/shard_map/all_to_all | solution.py:82
